TPU v7x, 256 devices: a whole 4x4x8 slice. The times are simulated.
256 devices in a mesh: cls: 8 (over z), dom: 32 (over x, y, core).
Axes of the slice: x: 4, y: 4, z: 8, core: 2. Of those that a mesh axis runs over, the one named last changes fastest.
Arguments:
- particles: bfloat16 [32768, 8192], P(('cls', 'dom')), may hold values from -6 to 6
- assign: int32 [32768, 1], P(('cls', 'dom')), may hold values from 0 to 15; in each aligned block of 128 rows (0 to 127, 128 to 255, ...) at most 16 rows name the same one
- inv_sigma: bfloat16 [32768], P(('cls', 'dom')), may hold values from 0.5 to 300, as said below
- projections: bfloat16 [16, 64, 8192], P('cls', 'dom'), may hold values from -0.0625 to 0.0625
Outputs:
- class_sums: float32 [16, 64, 8192], P('cls', 'dom')
- evidence: float32 [32768], P(('cls', 'dom'))
Inputs may be any that keep to these rules, and one draw needn't show every extreme that they name: `assign`: among the 128 particles of one device (aligned blocks of rows) no class is named more than 16 times, a bound that some block reaches. `inv_sigma`: each particle's noise precision, positive.
All inputs are finite; a program needn't handle non-finite values.
Results may differ from a plain program's by a relative error of at most 0.0023.
Values may be sent and summed in bfloat16 or wider, within the bound.
A program may use at most 64 MiB of HBM per device.

v0:
```python
import jax
import jax.numpy as jnp
from jax import lax
from jax.sharding import PartitionSpec as P


def on_device(particles, assign, inv_sigma, projections):
    local_rows = particles.shape[0]
    width = particles.shape[1]
    per_owner = projections.shape[0]
    own_rows = projections.shape[1]
    owners = lax.axis_size("cls")
    classes = per_owner * owners
    capacity = local_rows // 8
    class_id = assign[:, 0]
    one_hot = (class_id[:, None] == jnp.arange(classes, dtype=jnp.int32)[None, :]).astype(jnp.int32)
    before = jnp.cumsum(one_hot, axis=0) - one_hot
    ranking = jnp.sum(before * one_hot, axis=1)
    slot_index = (
        class_id % per_owner * (owners * capacity) + class_id // per_owner * capacity + ranking
    )
    slots = per_owner * owners * capacity
    source = (
        jnp.full((slots,), local_rows, jnp.int32)
        .at[slot_index]
        .set(jnp.arange(local_rows, dtype=jnp.int32))
    )
    padded = jnp.concatenate([particles, jnp.zeros((1, width), particles.dtype)], axis=0)
    padded_prec = jnp.concatenate([inv_sigma, jnp.zeros((1,), inv_sigma.dtype)], axis=0)
    packed = padded[source].reshape(per_owner, owners, capacity, width)
    packed_prec = padded_prec[source].reshape(per_owner, owners, capacity)
    arrived, arrived_prec = (
        lax.all_to_all(packed, "cls", split_axis=1, concat_axis=1, tiled=True),
        lax.all_to_all(packed_prec, "cls", split_axis=1, concat_axis=1, tiled=True),
    )
    arrived = arrived.reshape(per_owner, owners * capacity, width)
    precision = arrived_prec.reshape(per_owner, owners * capacity).astype(jnp.float32)
    piece = lax.all_gather(projections, "dom", axis=1, tiled=True)
    products = jnp.einsum("kmf,krf->kmr", arrived, piece, preferred_element_type=jnp.float32)
    halves = 0.5 * jnp.sum(jnp.square(piece.astype(jnp.float32)), axis=2)
    scores = precision[:, :, None] * (products - halves[:, None, :])
    is_live = precision > 0.0
    largest = jnp.max(scores, axis=2, keepdims=True)
    exponent = jnp.exp(scores - largest)
    totals = jnp.sum(exponent, axis=2, keepdims=True)
    weights = jnp.where(is_live[:, :, None], exponent / totals, 0.0).astype(jnp.bfloat16)
    log_total = jnp.where(is_live, largest[:, :, 0] + jnp.log(totals[:, :, 0]), 0.0)
    pieces = []
    for member in range(per_owner):

        def class_term(start, count, member=member):
            window = weights[member]
            return lax.dot_general(
                window,
                arrived[member],
                (((0,), (0,)), ((), ())),
                preferred_element_type=jnp.float32,
            )

        pieces.append(
            lax.psum_scatter(
                class_term(jnp.int32(0), own_rows * lax.axis_size("dom")),
                "dom",
                scatter_dimension=0,
                tiled=True,
            )
        )
    class_sums = jnp.stack(pieces, axis=0)
    returned = lax.all_to_all(
        log_total.reshape(per_owner, owners, capacity),
        "cls",
        split_axis=1,
        concat_axis=1,
        tiled=True,
    )
    evidence = returned.reshape(slots)[slot_index]
    return (class_sums, evidence)


def solution(mesh):
    return jax.shard_map(
        on_device,
        mesh=mesh,
        in_specs=(
            P(("cls", "dom"), None),
            P(("cls", "dom"), None),
            P(("cls", "dom")),
            P("cls", "dom", None),
        ),
        out_specs=(P("cls", "dom", None), P(("cls", "dom"))),
        check_vma=False,
    )
```

profile of v0, /device:TPU:1, one launch (start us, length us, event | category | flops | bytes accessed | tf_op | source)
XLA Modules:
  0.0 275.4 jit_solution(17666839986400821745)
XLA Ops:
  7.2 0.7 fusion.8
  7.9 0.2 reduce_window_sum.11
  8.1 0.8 select_reduce_fusion
  8.9 0.7 fusion.15
  9.6 1.0 scatter_custom_fusion
  10.6 0.7 pad_maximum_fusion.1
  11.3 1.9 gather_fusion
  13.2 0.1 reshape.43
  13.2 0.6 copy.27
  13.8 9.0 %all-to-all-start = ((bf16[2,8,16]{2,0,1:T(2,128)(2,1)}), bf16[2,8,16]{2,0,1:T(2,128)(2,1)S(1)}, u32[]{:S(2)}, u32[]{:S(2)}) async-start(bf16[2,8,16]{2,0,1:T(2,128)(2,1)} %copy.27), calls=%async_computation | async-start | bytes 8192 | tf_op jit(solution)/shard_map/all_to_all | solution.py:34
  22.8 1.8 concatenate.7
  24.7 5.1 %gather_fusion.1 = bf16[256,8192]{1,0:T(8,128)(2,1)} fusion(bf16[129,8192]{1,0:T(8,128)(2,1)S(1)} %concatenate.7, s32[1024]{0:T(1024)S(1)} %pad_clamp_fusion.1), kind=kCustom, calls=%fused_computation.1 | custom fusion | bytes 8389632 | tf_op jit(solution)/shard_map/gather | solution.py:30
  29.8 4.6 %copy.29 = bf16[2,8,16,8192]{3,2,0,1:T(8,128)(2,1)} copy(bf16[2,8,16,8192]{3,2,1,0:T(8,128)(2,1)} %bitcast.25) | data formatting | bytes 8388608 | tf_op jit(solution)/shard_map/reshape | solution.py:30
  34.4 0.0 copy-start.1
  34.4 0.0 all-to-all-done
  34.4 6.8 %all-to-all-start.1 = ((bf16[2,8,16,8192]{3,2,0,1:T(8,128)(2,1)}), bf16[2,8,16,8192]{3,2,0,1:T(8,128)(2,1)}, u32[]{:S(2)}, u32[]{:S(2)}) async-start(bf16[2,8,16,8192]{3,2,0,1:T(8,128)(2,1)} %copy.29), calls=%async_computation.1 | async-start | bytes 8388608 | tf_op jit(solution)/shard_map/all_to_all | solution.py:33
  41.2 0.0 all-gather.2.cloned.1.call-start
  41.2 0.0 copy-done.1
  41.2 0.7 copy.31
  41.9 0.0 all-gather.2.cloned.1.call-update
  42.0 0.0 all-reduce.6.cloned.1.call-start
  42.0 0.1 reshape.47
  42.1 54.5 %all-gather.2.cloned.1.call-done = bf16[2,64,8192]{2,0,1:T(2,128)(2,1)} async-done(((bf16[2,2,8192]{2,0,1:T(2,128)(2,1)}), bf16[2,64,8192]{2,0,1:T(2,128)(2,1)}) %all-gather.2.cloned.1.call-update) | async-done | bytes 2097168 | tf_op jit(solution)/shard_map/all_gather | solution.py:38
  96.6 3.8 %multiply_reduce_fusion = f32[2,64]{0,1:T(8,128)S(1)} fusion(bf16[2,64,8192]{2,0,1:T(2,128)(2,1)} %all-gather.2.cloned.1.call-done), kind=kLoop, calls=%fused_computation.4 | loop fusion | flops 3145600 | bytes 2097664 | tf_op jit(solution)/shard_map/reduce_sum | solution.py:40
  100.4 0.1 copy.33
  100.5 0.0 copy-start
  100.5 37.5 %all-to-all-done.1 = bf16[2,8,16,8192]{3,2,0,1:T(8,128)(2,1)} async-done(((bf16[2,8,16,8192]{3,2,0,1:T(8,128)(2,1)}), bf16[2,8,16,8192]{3,2,0,1:T(8,128)(2,1)}, u32[]{:S(2)}, u32[]{:S(2)}) %all-to-all-start.1) | async-done | bytes 4194336 | tf_op jit(solution)/shard_map/all_to_all | solution.py:33
  138.0 2.5 copy.30
  140.5 0.0 copy-done
  140.5 1.9 fusion.19
  142.5 2.7 fusion.18
  145.1 1.8 fusion.11
  146.9 1.8 fusion.10
  148.7 0.0 copy-start.2
  148.7 0.0 all-reduce.6.cloned.1.call-update
  148.7 0.1 add.45
  148.8 0.6 copy.34
  149.4 3.3 %all-to-all-start.2 = ((f32[2,8,16]{2,0,1:T(2,128)}), f32[2,8,16]{2,0,1:T(2,128)S(1)}, u32[]{:S(2)}, u32[]{:S(2)}) async-start(f32[2,8,16]{2,0,1:T(2,128)} %copy.34), calls=%async_computation.2 | async-start | bytes 16384 | tf_op jit(solution)/shard_map/all_to_all | solution.py:69
  152.8 0.0 copy-done.2
  152.8 0.6 dynamic-slice
  154.0 5.3 %all-to-all-done.2 = f32[2,8,16]{2,0,1:T(2,128)S(1)} async-done(((f32[2,8,16]{2,0,1:T(2,128)}), f32[2,8,16]{2,0,1:T(2,128)S(1)}, u32[]{:S(2)}, u32[]{:S(2)}) %all-to-all-start.2) | async-done | bytes 1056 | tf_op jit(solution)/shard_map/all_to_all | solution.py:69
  159.3 0.1 reshape.46
  159.4 1.8 gather_fusion.2
  161.1 105.6 %all-reduce.6.cloned.1.call-done = (f32[64,8192]{1,0:T(8,128)}, f32[64,8192]{1,0:T(8,128)}) async-done(((f32[64,8192]{1,0:T(8,128)}, f32[64,8192]{1,0:T(8,128)}), (f32[64,8192]{1,0:T(8,128)}, f32[64,8192]{1,0:T(8,128)})) %all-reduce.6.cloned.1.call-update) | async-done | bytes 4194320
  266.8 1.1 dynamic-slice_bitcast_fusion
  267.8 0.7 pad_maximum_fusion
  (12 shorter events, 0.1 us)
Async XLA Ops:
  13.8 20.6 %all-to-all-start = ((bf16[2,8,16]{2,0,1:T(2,128)(2,1)}), bf16[2,8,16]{2,0,1:T(2,128)(2,1)S(1)}, u32[]{:S(2)}, u32[]{:S(2)}) async-start(bf16[2,8,16]{2,0,1:T(2,128)(2,1)} %copy.27), calls=%async_computation | async-start | bytes 8192 | tf_op jit(solution)/shard_map/all_to_all | solution.py:34
  34.4 6.8 %copy-start.1 = (bf16[2,2,8192]{2,1,0:T(2,128)(2,1)S(1)}, bf16[2,2,8192]{2,1,0:T(2,128)(2,1)}, u32[]{:S(2)}) copy-start(bf16[2,2,8192]{2,1,0:T(2,128)(2,1)} %param.7) | copy-start | bytes 196612
  34.4 103.6 %all-to-all-start.1 = ((bf16[2,8,16,8192]{3,2,0,1:T(8,128)(2,1)}), bf16[2,8,16,8192]{3,2,0,1:T(8,128)(2,1)}, u32[]{:S(2)}, u32[]{:S(2)}) async-start(bf16[2,8,16,8192]{3,2,0,1:T(8,128)(2,1)} %copy.29), calls=%async_computation.1 | async-start | bytes 8388608 | tf_op jit(solution)/shard_map/all_to_all | solution.py:33
  41.2 55.4 %all-gather.2.cloned.1.call-start = ((), (), s32[]{:S(2)}) async-start(), calls=%async_computation.3 | async-start | bytes 2162688 | tf_op jit(solution)/shard_map/all_gather | solution.py:38
  42.0 224.8 %all-reduce.6.cloned.1.call-start = ((), (), s32[]{:S(2)}) async-start(), calls=%async_computation.4 | async-start | bytes 8388608
  100.5 40.0 %copy-start = (bf16[2,64,8192]{2,0,1:T(2,128)(2,1)S(1)}, bf16[2,64,8192]{2,0,1:T(2,128)(2,1)}, u32[]{:S(2)}) copy-start(bf16[2,64,8192]{2,0,1:T(2,128)(2,1)} %all-gather.2.cloned.1.call-done) | copy-start | bytes 6291460
  148.7 4.1 %copy-start.2 = (u32[256]{0:T(256)S(1)}, u32[256]{0:T(256)}, u32[]{:S(2)}) copy-start(u32[256]{0:T(256)} %constant.61) | copy-start | bytes 3076
  149.4 9.9 %all-to-all-start.2 = ((f32[2,8,16]{2,0,1:T(2,128)}), f32[2,8,16]{2,0,1:T(2,128)S(1)}, u32[]{:S(2)}, u32[]{:S(2)}) async-start(f32[2,8,16]{2,0,1:T(2,128)} %copy.34), calls=%async_computation.2 | async-start | bytes 16384 | tf_op jit(solution)/shard_map/all_to_all | solution.py:69
Sparse Core Ops, SparseCore 0:
  45.1 51.4 all-gather.1
  148.8 117.9 all-reduce.5
where the time goes:
time: 276 us; the launch traced here: 275 us
  waiting for transfers between devices  203 us (74%)
  local copies, waits for them, and re-layouts  25.3 us (9%)
  starting transfers between devices  19.2 us (7%)
  between operations  14.8 us (5%)
  other arithmetic  7.75 us (3%)
  matrix products  5.42 us (2%)
    unnamed x3, waiting for transfers between devices  106 us
    all_gather x1, waiting for transfers between devices, on_device(): piece = lax.all_gather(projections, 'dom', axis=1, tiled=True)  54.5 us
    all_to_all x1, waiting for transfers between devices, on_device(): lax.all_to_all(packed, 'cls', split_axis=1, concat_axis=1, tiled=True)  37.5 us
    all_to_all x1, starting transfers between devices, on_device(): lax.all_to_all(packed_prec, 'cls', split_axis=1, concat_axis=1, tiled=True)  9 us
    all_to_all x1, starting transfers between devices, on_device(): lax.all_to_all(packed, 'cls', split_axis=1, concat_axis=1, tiled=True)  6.78 us
  transfers between devices with their start and end apart: 5, of which 4 were waited for; matrix products, arithmetic and copies ran while one was open for 7% of the time, Pallas kernels for 0%

commit v1 on v0

v1 whole, which is shorter than its diff:
```python
import functools

import jax
import jax.numpy as jnp
from jax import lax
from jax.experimental import pallas as pl
from jax.experimental.pallas import tpu as pltpu
from jax.sharding import PartitionSpec as P

MESH = pl.DeviceIdType.MESH
TWIST = True
NX, NY, NZ = 4, 4, 8
F32 = jnp.float32
BF16 = jnp.bfloat16


def _mod(v, n):
    return lax.rem(v + 2 * n, n)


def _device(x, y, z, c):
    return (_mod(z, NZ), (_mod(x, NX) * NY + _mod(y, NY)) * 2 + c)


def _shift(k):
    i, j = lax.div(k, 4), lax.rem(k, 4)
    if not TWIST:
        return i, j, 0
    low_i, low_j = jnp.where(i == 3, -1, i), jnp.where(j == 3, -1, j)
    both = jnp.where(jnp.minimum(low_i, low_j) > 0, jnp.minimum(low_i, low_j), -1)
    flat = (low_i == 0) | (low_j == 0) | (low_i + low_j == 0)
    dz = jnp.where(flat, 0, both)
    return i - dz, j - dz, dz


def kernel(
    x_ref, a_ref, s_ref, j_ref, out_ref, ev_ref,
    X, A, J1, ASM, PJ, H, T, SS, SR, WS, WB, WM, ACC, RS, RR, FS,
    lsem, xs, xr, as_, ar, js, jr, gs, gr, ss, sr, ws, wr, rs, rr, fs, fr,
):
    d, z = lax.axis_index("dom"), lax.axis_index("cls")
    c = lax.rem(d, 2)
    y = lax.rem(lax.div(d, 2), NY)
    x = lax.div(d, 2 * NY)
    t = z if TWIST else 0

    def colour(i, j, core):
        return (_mod(x + t + i, NX) * NY + _mod(y + t + j, NY)) * 2 + core

    def cols(s):
        return pl.ds(pl.multiple_of(s * 256, 256), 256)

    def peer(k, core, sign=1):
        dx, dy, dz = _shift(k)
        return _device(x + sign * dx, y + sign * dy, z + sign * dz, core)

    def plane_peer(k, core):
        return _device(x + lax.div(k, 4), y + lax.rem(k, 4), z, core)

    def column_peer(h):
        if TWIST:
            return _device(x - h + 8, y - h + 8, z + h, c)
        return _device(x, y, z + h, c)

    def each(fn):
        fn(0, 1 - c)

        def body(k, _):
            fn(k, 0)
            fn(k, 1)
            return 0

        lax.fori_loop(1, 16, body, 0)

    barrier = pltpu.get_barrier_semaphore()

    def greet(device):
        pl.semaphore_signal(barrier, inc=1, device_id=device, device_id_type=MESH)

    each(lambda k, core: greet(plane_peer(k, core)))
    for h in range(1, NZ):
        greet(column_peer(h))
    greeted = 31 + 7
    if TWIST:
        for dx, dy, dz in ((0, 0, 1), (1, 0, 1), (0, 1, 1), (0, 0, 2)):
            for sign in (1, -1):
                for core in (0, 1):
                    greet(_device(x + sign * dx, y + sign * dy, z + sign * dz, core))
                    greeted += 1
    pl.semaphore_wait(barrier, greeted)

    def send_j(k, core):
        s = colour(lax.div(k, 4), lax.rem(k, 4), core)
        return pltpu.make_async_remote_copy(
            src_ref=j_ref.at[:, :, cols(s)], dst_ref=J1.at[d],
            send_sem=js.at[2 * k + core], recv_sem=jr.at[d],
            device_id=plane_peer(k, core), device_id_type=MESH)

    def recv_j(q):
        return pltpu.make_async_remote_copy(
            src_ref=J1.at[q], dst_ref=J1.at[q], send_sem=js.at[q], recv_sem=jr.at[q],
            device_id=plane_peer(1, c), device_id_type=MESH)

    def send_x(k, core):
        s = colour(lax.div(k, 4), lax.rem(k, 4), core)
        return pltpu.make_async_remote_copy(
            src_ref=x_ref.at[:, cols(s)], dst_ref=X.at[2 * k + c],
            send_sem=xs.at[2 * k + core], recv_sem=xr.at[2 * k + c],
            device_id=peer(k, core), device_id_type=MESH)

    def send_a(k, core):
        return pltpu.make_async_remote_copy(
            src_ref=a_ref, dst_ref=A.at[2 * k + c],
            send_sem=as_.at[2 * k + core], recv_sem=ar.at[2 * k + c],
            device_id=peer(k, core), device_id_type=MESH)

    def recv(buf, ssem, rsem, slot):
        return pltpu.make_async_remote_copy(
            src_ref=buf.at[slot], dst_ref=buf.at[slot], send_sem=ssem.at[slot], recv_sem=rsem.at[slot],
            device_id=peer(1, c), device_id_type=MESH)

    def send_s(k, core):
        return pltpu.make_async_remote_copy(
            src_ref=SS.at[2 * k + core], dst_ref=SR.at[2 * k + c],
            send_sem=ss.at[2 * k + core], recv_sem=sr.at[2 * k + c],
            device_id=peer(k, core, -1), device_id_type=MESH)

    def send_w(k, core):
        return pltpu.make_async_remote_copy(
            src_ref=WS, dst_ref=WB.at[2 * k + c],
            send_sem=ws.at[2 * k + core], recv_sem=wr.at[2 * k + c],
            device_id=peer(k, core), device_id_type=MESH)

    def send_g(h):
        return pltpu.make_async_remote_copy(
            src_ref=PJ.at[z], dst_ref=PJ.at[z], send_sem=gs.at[h], recv_sem=gr.at[z],
            device_id=column_peer(h), device_id_type=MESH)

    def recv_g(p):
        return pltpu.make_async_remote_copy(
            src_ref=PJ.at[p], dst_ref=PJ.at[p], send_sem=gs.at[p], recv_sem=gr.at[p],
            device_id=column_peer(1), device_id_type=MESH)

    def send_r(h):
        return pltpu.make_async_remote_copy(
            src_ref=RS.at[h], dst_ref=RR.at[h], send_sem=rs.at[h], recv_sem=rr.at[h],
            device_id=column_peer(h), device_id_type=MESH)

    def send_f(k, core):
        q = (_mod(x + lax.div(k, 4), NX) * NY + _mod(y + lax.rem(k, 4), NY)) * 2 + core
        return pltpu.make_async_remote_copy(
            src_ref=FS.at[q], dst_ref=out_ref.at[:, :, cols(colour(0, 0, c))],
            send_sem=fs.at[2 * k + core], recv_sem=fr.at[2 * k + c],
            device_id=plane_peer(k, core), device_id_type=MESH)

    def recv_f(k, core):
        return pltpu.make_async_remote_copy(
            src_ref=FS.at[0], dst_ref=out_ref.at[:, :, cols(colour(-lax.div(k, 4), -lax.rem(k, 4), core))],
            send_sem=fs.at[2 * k + core], recv_sem=fr.at[2 * k + core],
            device_id=plane_peer(k, core), device_id_type=MESH)

    mine = colour(0, 0, c)
    own_x = pltpu.make_async_copy(x_ref.at[:, cols(mine)], X.at[c], lsem.at[0])
    own_j = pltpu.make_async_copy(j_ref.at[:, :, cols(mine)], J1.at[d], lsem.at[1])
    own_j.start()
    each(lambda k, core: send_j(k, core).start())
    each(lambda k, core: send_a(k, core).start())
    own_x.start()
    each(lambda k, core: send_x(k, core).start())
    A[c] = a_ref[...]

    own_j.wait()
    def wait_j(q, _):
        @pl.when(q != d)
        def _():
            recv_j(q).wait_recv()
        return 0
    lax.fori_loop(0, 32, wait_j, 0)
    for q in range(32):
        for kk in range(2):
            ASM[kk * 64 + 2 * q : kk * 64 + 2 * q + 2, :] = J1[q, kk].astype(F32)
    PJ[z] = ASM[...].astype(BF16)
    for h in range(1, NZ):
        send_g(h).start()

    def wait_g(p, _):
        @pl.when(p != z)
        def _():
            recv_g(p).wait_recv()
        v = PJ[p].astype(F32)
        half = 0.5 * jnp.sum(v * v, axis=1, keepdims=True)
        H[p] = jnp.broadcast_to(half, (128, 128))
        return 0
    lax.fori_loop(0, NZ, wait_g, 0)

    own_x.wait()

    def wait_slot(k, core, buf, ssem, rsem):
        @pl.when((k != 0) | (c != core))
        def _():
            recv(buf, ssem, rsem, 2 * k + core).wait_recv()

    def score(k, _):
        for core in range(2):
            wait_slot(k, core, X, xs, xr)
            wait_slot(k, core, A, as_, ar)
        rows = X[pl.ds(2 * k, 2)].reshape(256, 256)
        T[...] = lax.dot_general(
            PJ[...].reshape(1024, 256), rows, (((1,), (1,)), ((), ())), preferred_element_type=F32)
        for core in range(2):
            ids = jnp.broadcast_to(A[2 * k + core], (64, 128))
            total = jnp.zeros((64, 128), F32)
            for m in range(16):
                part = T[m * 64 : (m + 1) * 64, core * 128 : (core + 1) * 128]
                half = H[m // 2, (m % 2) * 64 : (m % 2) * 64 + 64, :]
                total = jnp.where(ids == m, part - half, total)
            SS[2 * k + core] = total
        for core in range(2):
            @pl.when((k != 0) | (c != core))
            def _():
                send_s(k, core).start()
        return 0
    lax.fori_loop(0, 16, score, 0)

    def gather(k, total):
        for core in range(2):
            recv(SR, ss, sr, 2 * k + core).wait_recv()
            total = total + SR[2 * k + core]
        return total
    recv(SR, ss, sr, 1 - c).wait_recv()
    total = lax.fori_loop(1, 16, gather, SS[c] + SR[1 - c])
    scores = total * s_ref[...].astype(F32)
    largest = jnp.max(scores, axis=0, keepdims=True)
    expo = jnp.exp(scores - largest)
    sums = jnp.sum(expo, axis=0, keepdims=True)
    weight = (expo / sums).astype(BF16)
    WS[...] = weight
    WB[c] = weight
    each(lambda k, core: send_w(k, core).start())
    ev_ref[...] = largest + jnp.log(sums)

    ACC[...] = jnp.zeros_like(ACC)

    def accumulate(k, _):
        for core in range(2):
            wait_slot(k, core, WB, ws, wr)
        for core in range(2):
            ids = jnp.broadcast_to(A[2 * k + core], (64, 128))
            w = WB[2 * k + core].astype(F32)
            for m in range(16):
                WM[m * 64 : (m + 1) * 64, core * 128 : (core + 1) * 128] = jnp.where(ids == m, w, 0.0).astype(BF16)
        rows = X[pl.ds(2 * k, 2)].reshape(256, 256)
        ACC[...] += jnp.dot(WM[...], rows, preferred_element_type=F32)
        return 0
    lax.fori_loop(0, 16, accumulate, 0)

    for h in range(1, NZ):
        p = _mod(z + h, NZ)
        RS[h] = ACC[pl.ds(pl.multiple_of(p * 128, 128), 128), :].astype(BF16)
        send_r(h).start()
    final = ACC[pl.ds(pl.multiple_of(z * 128, 128), 128), :]
    for h in range(1, NZ):
        send_r(h).wait_recv()
        final = final + RR[h].astype(F32)
    ASM[...] = final
    for q in range(32):
        for kk in range(2):
            FS[q, kk] = ASM[kk * 64 + 2 * q : kk * 64 + 2 * q + 2, :]
    each(lambda k, core: send_f(k, core).start())
    out_ref[:, :, cols(mine)] = FS[d]
    each(lambda k, core: recv_f(k, core).wait_recv())

    for send in (send_j, send_a, send_x, send_s, send_w, send_f):
        each(lambda k, core, send=send: send(k, core).wait_send())
    for h in range(1, NZ):
        send_g(h).wait_send()
        send_r(h).wait_send()


def on_device(particles, assign, inv_sigma, projections):
    dma = pltpu.SemaphoreType.DMA
    vmem = pltpu.VMEM
    sums, evidence = pl.pallas_call(
        kernel,
        name="estep",
        out_shape=(
            jax.ShapeDtypeStruct((2, 2, 8192), F32),
            jax.ShapeDtypeStruct((1, 128), F32),
        ),
        in_specs=[
            pl.BlockSpec(memory_space=pl.ANY),
            pl.BlockSpec(memory_space=pltpu.VMEM),
            pl.BlockSpec(memory_space=pltpu.VMEM),
            pl.BlockSpec(memory_space=pl.ANY),
        ],
        out_specs=(
            pl.BlockSpec(memory_space=pltpu.VMEM),
            pl.BlockSpec(memory_space=pltpu.VMEM),
        ),
        scratch_shapes=[
            vmem((32, 128, 256), BF16),
            vmem((32, 1, 128), jnp.int32),
            vmem((32, 2, 2, 256), BF16),
            vmem((128, 256), F32),
            vmem((8, 128, 256), BF16),
            vmem((8, 128, 128), F32),
            vmem((1024, 256), F32),
            vmem((32, 64, 128), F32),
            vmem((32, 64, 128), F32),
            vmem((64, 128), BF16),
            vmem((32, 64, 128), BF16),
            vmem((1024, 256), BF16),
            vmem((1024, 256), F32),
            vmem((8, 128, 256), BF16),
            vmem((8, 128, 256), BF16),
            vmem((32, 2, 2, 256), F32),
            dma((2,)),
            dma((32,)), dma((32,)),
            dma((32,)), dma((32,)),
            dma((32,)), dma((32,)),
            dma((8,)), dma((8,)),
            dma((32,)), dma((32,)),
            dma((32,)), dma((32,)),
            dma((8,)), dma((8,)),
            dma((32,)), dma((32,)),
        ],
        compiler_params=pltpu.CompilerParams(collective_id=0, has_side_effects=True),
    )(particles, assign.reshape(1, 128), inv_sigma.reshape(1, 128), projections)
    return sums, evidence.reshape(128)


def solution(mesh):
    return jax.shard_map(
        on_device,
        mesh=mesh,
        in_specs=(
            P(("cls", "dom"), None),
            P(("cls", "dom"), None),
            P(("cls", "dom")),
            P("cls", "dom", None),
        ),
        out_specs=(P("cls", "dom", None), P(("cls", "dom"))),
        check_vma=False,
    )
```

time: 276 us -> 92 us (0.33)
  waiting for transfers between devices: 203 us -> 0 us
  Pallas kernels: 0 us -> 88.5 us
  local copies, waits for them, and re-layouts: 25.3 us -> 2.74 us
  starting transfers between devices: 19.2 us -> 0 us
  between operations: 14.8 us -> 0.64 us
  other arithmetic: 7.75 us -> 0 us
  matrix products: 5.42 us -> 0 us
    unnamed x3 -> x0, waiting for transfers between devices: 106 us -> none
    pallas_call x0 -> x1, Pallas kernels: none -> 88.5 us  [on_device(): pl.pallas_call(kernel, name='estep', out_shape=(jax.ShapeDtypeStruct((2,...]
    all_gather x1 -> x0, waiting for transfers between devices: 54.5 us -> none  [on_device(): piece = lax.all_gather(projections, 'dom', axis=1, tiled=True)]
    all_to_all x3 -> x0, waiting for transfers between devices: 42.8 us -> none  [the longest x1 37.5 us: on_device(): lax.all_to_all(packed, 'cls', split_axis=1, concat_axis=1, tiled=True)]
    all_to_all x3 -> x0, starting transfers between devices: 19.1 us -> none  [the longest x1 9 us: on_device(): lax.all_to_all(packed_prec, 'cls', split_axis=1, concat_axis=1, tiled=True)]
    gather x3 -> x0, local copies, waits for them, and re-layouts: 8.77 us -> none  [the longest x1 5.13 us: on_device(): packed = padded[source].reshape(per_owner, owners, capacity, width)]
    dot_general x3 -> x0, matrix products: 5.42 us -> none  [the longest x2 3.53 us: class_term(): lax.dot_general(window, arrived[member], (((0,), (0,)), ((), ())), prefer...]
    reshape x4 -> x0, local copies, waits for them, and re-layouts: 5.36 us -> none  [the longest x1 4.59 us: on_device(): packed = padded[source].reshape(per_owner, owners, capacity, width)]
  transfers between devices with their start and end apart: 5 -> 0, of which waited for: 4 -> 0; matrix products, arithmetic and copies ran while one was open for 7% -> 0% of each run, Pallas kernels for 0% -> 0%
where the time goes in v1:
time: 92 us; the launch traced here: 91.8 us
  Pallas kernels  88.5 us (96%)
  local copies, waits for them, and re-layouts  2.74 us (3%)
    pallas_call x1, Pallas kernels, on_device(): pl.pallas_call(kernel, name='estep', out_shape=(jax.ShapeDtypeStruct((2,...  88.5 us
    unnamed x2, local copies, waits for them, and re-layouts  2.74 us

profile of v1, /device:TPU:1, one launch (start us, length us, event | category | flops | bytes accessed | tf_op | source)
XLA Modules:
  0.0 91.8 jit_solution(18013832570925757466)
XLA Ops:
  0.6 88.5 %estep.1 = (f32[2,2,8192]{2,1,0:T(2,128)}, f32[1,128]{1,0:T(1,128)}) custom-call(bf16[128,8192]{1,0:T(8,128)(2,1)} %x_ref.1, s32[1,128]{1,0:T(1,128)} %bitcast.3, bf16[1,128]{1,0:T(2,128)(2,1)} %bitcast.4, bf16[2,2,8192]{2,1,0:T(2,128)(2,1)} %j_ref.1), custom_call_target="tpu_custom_call" | custom-call | tf_op jit(solution)/shard_map/estep/pallas_call | solution.py:283
  89.1 1.6 %copy.8 = f32[2,2,8192]{2,1,0:T(2,128)} copy(f32[2,2,8192]{2,1,0:T(2,128)} %get-tuple-element.8) | data formatting | bytes 262144
  90.7 1.2 %copy.9 = f32[128]{0:T(128)} copy(f32[128]{0:T(128)} %bitcast.5) | data formatting | bytes 1024

commit v2 on v1

v2 whole, which is shorter than its diff:
```python
import functools

import jax
import jax.numpy as jnp
from jax import lax
from jax.experimental import pallas as pl
from jax.experimental.pallas import tpu as pltpu
from jax.sharding import PartitionSpec as P

MESH = pl.DeviceIdType.MESH
TWIST = True
EARLY = 7
ORDER = (2, 6, 3, 5, 4, 1, 7)
NX, NY, NZ = 4, 4, 8
F32 = jnp.float32
BF16 = jnp.bfloat16


def _mod(v, n):
    return v % n if isinstance(v, int) else v & (n - 1)


def _device(x, y, z, c):
    return (_mod(z, NZ), (_mod(x, NX) * NY + _mod(y, NY)) * 2 + c)


def _table():
    table = []
    for i in (0, 1, 2, -1):
        for j in (0, 1, 2, -1):
            dz = 0
            if TWIST and i and j and i + j:
                dz = min(i, j) if min(i, j) > 0 else -1
            table.append((i - dz, j - dz, dz))
    return table


TABLE = _table()


def _shift(k):
    if isinstance(k, int):
        return TABLE[k]
    i, j = k >> 2, k & 3
    if not TWIST:
        return i, j, 0
    low_i, low_j = jnp.where(i == 3, -1, i), jnp.where(j == 3, -1, j)
    both = jnp.where(jnp.minimum(low_i, low_j) > 0, jnp.minimum(low_i, low_j), -1)
    flat = (low_i == 0) | (low_j == 0) | (low_i + low_j == 0)
    dz = jnp.where(flat, 0, both)
    return i - dz, j - dz, dz


def kernel(
    x_ref, a_ref, s_ref, j_ref, out_ref, ev_ref,
    X, A, J1, ASM, PJ, H, T, SS, SR, WS, WB, WM, ACC, RS, RR, FS,
    lsem, xs, xr, as_, ar, js, jr, gs, gr, ss, sr, ws, wr, rs, rr, fs, fr,
):
    d, z = lax.axis_index("dom"), lax.axis_index("cls")
    c = d & 1
    y = (d >> 1) & 3
    x = d >> 3
    t = z if TWIST else 0

    def colour(i, j, core):
        return (_mod(x + t + i, NX) * NY + _mod(y + t + j, NY)) * 2 + core

    def cols(s):
        return pl.ds(pl.multiple_of(s * 256, 256), 256)

    def peer(k, core, sign=1):
        dx, dy, dz = _shift(k)
        return _device(x + sign * dx, y + sign * dy, z + sign * dz, core)

    def plane_peer(k, core):
        return _device(x + (k >> 2), y + (k & 3), z, core)

    def column_peer(h):
        if TWIST:
            return _device(x - h + 8, y - h + 8, z + h, c)
        return _device(x, y, z + h, c)

    def each(fn):
        fn(0, 1 - c)

        for k in range(1, 16):
            fn(k, 0)
            fn(k, 1)

    barrier = pltpu.get_barrier_semaphore()

    def greet(device):
        pl.semaphore_signal(barrier, inc=1, device_id=device, device_id_type=MESH)

    each(lambda k, core: greet(plane_peer(k, core)))
    for h in range(1, NZ):
        greet(_device(x, y, z + h, c))
    greeted = 31 + 7
    if TWIST:
        for dx, dy, dz in ((0, 0, 1), (1, 0, 1), (0, 1, 1), (0, 0, 2)):
            for sign in (1, -1):
                for core in (0, 1):
                    greet(_device(x + sign * dx, y + sign * dy, z + sign * dz, core))
                    greeted += 1
    pl.semaphore_wait(barrier, greeted)

    def send_j(k, core):
        s = colour((k >> 2), (k & 3), core)
        return pltpu.make_async_remote_copy(
            src_ref=j_ref.at[:, :, cols(s)], dst_ref=J1.at[d],
            send_sem=js, recv_sem=jr,
            device_id=plane_peer(k, core), device_id_type=MESH)

    def send_x(k, core):
        s = colour((k >> 2), (k & 3), core)
        return pltpu.make_async_remote_copy(
            src_ref=x_ref.at[:, cols(s)], dst_ref=X.at[2 * k + c],
            send_sem=xs, recv_sem=xr.at[k],
            device_id=peer(k, core), device_id_type=MESH)

    def send_a(k, core):
        return pltpu.make_async_remote_copy(
            src_ref=a_ref, dst_ref=A.at[2 * k + c],
            send_sem=as_, recv_sem=ar,
            device_id=peer(k, core), device_id_type=MESH)

    def all_of(buf, ssem, rsem, n=31):
        return pltpu.make_async_remote_copy(
            src_ref=buf.at[pl.ds(0, n)], dst_ref=buf.at[pl.ds(0, n)], send_sem=ssem, recv_sem=rsem,
            device_id=plane_peer(0, 1 - c), device_id_type=MESH)

    def send_s(k, core):
        return pltpu.make_async_remote_copy(
            src_ref=SS.at[2 * k + core], dst_ref=SR.at[2 * k + c],
            send_sem=ss, recv_sem=sr,
            device_id=peer(k, core, -1), device_id_type=MESH)

    def send_w(k, core):
        return pltpu.make_async_remote_copy(
            src_ref=WS, dst_ref=WB.at[2 * k + c],
            send_sem=ws, recv_sem=wr,
            device_id=peer(k, core), device_id_type=MESH)

    def send_g(h):
        return pltpu.make_async_remote_copy(
            src_ref=PJ.at[z], dst_ref=PJ.at[z], send_sem=gs, recv_sem=gr,
            device_id=column_peer(h), device_id_type=MESH)

    def send_r(h):
        return pltpu.make_async_remote_copy(
            src_ref=RS.at[h], dst_ref=RR.at[h], send_sem=rs, recv_sem=rr,
            device_id=column_peer(h), device_id_type=MESH)

    def send_f(k, core):
        q = (_mod(x + (k >> 2), NX) * NY + _mod(y + (k & 3), NY)) * 2 + core
        return pltpu.make_async_remote_copy(
            src_ref=FS.at[q], dst_ref=out_ref.at[:, :, cols(colour(0, 0, c))],
            send_sem=fs, recv_sem=fr,
            device_id=plane_peer(k, core), device_id_type=MESH)

    mine = colour(0, 0, c)
    own_x = pltpu.make_async_copy(x_ref.at[:, cols(mine)], X.at[c], lsem.at[0])
    own_j = pltpu.make_async_copy(j_ref.at[:, :, cols(mine)], J1.at[d], lsem.at[1])
    own_j.start()
    each(lambda k, core: send_j(k, core).start())
    each(lambda k, core: send_a(k, core).start())
    own_x.start()

    def start_x(lo, hi):
        for k in range(lo, hi):
            send_x(k, 0).start()
            send_x(k, 1).start()

    send_x(0, 1 - c).start()
    start_x(1, EARLY)
    A[c] = a_ref[...]

    own_j.wait()
    all_of(J1, js, jr).wait_recv()
    for q in range(32):
        for kk in range(2):
            ASM[kk * 64 + 2 * q : kk * 64 + 2 * q + 2, :] = J1[q, kk].astype(F32)
    PJ[z] = ASM[...].astype(BF16)
    for h in ORDER:
        send_g(h).start()
    start_x(EARLY, 16)

    all_of(PJ, gs, gr, 7).wait_recv()

    def halve(p, _):
        v = PJ[p].astype(F32)
        half = 0.5 * jnp.sum(v * v, axis=1, keepdims=True)
        H[p] = jnp.broadcast_to(half, (128, 128))
        return 0
    lax.fori_loop(0, NZ, halve, 0)

    own_x.wait()

    all_of(A, as_, ar).wait_recv()

    def score(k, _):
        @pl.when(k == 0)
        def _():
            all_of(X, xs, xr.at[0], 1).wait_recv()

        @pl.when(k != 0)
        def _():
            all_of(X, xs, xr.at[k], 2).wait_recv()

        rows = X[pl.ds(2 * k, 2)].reshape(256, 256)
        T[...] = lax.dot_general(
            PJ[...].reshape(1024, 256), rows, (((1,), (1,)), ((), ())), preferred_element_type=F32)
        for core in range(2):
            ids = jnp.broadcast_to(A[2 * k + core], (64, 128))
            total = jnp.zeros((64, 128), F32)
            for m in range(16):
                part = T[m * 64 : (m + 1) * 64, core * 128 : (core + 1) * 128]
                half = H[m // 2, (m % 2) * 64 : (m % 2) * 64 + 64, :]
                total = jnp.where(ids == m, part - half, total)
            SS[2 * k + core] = total
        for core in range(2):
            @pl.when((k != 0) | (c != core))
            def _():
                send_s(k, core).start()
        return 0
    lax.fori_loop(0, 16, score, 0)

    all_of(SR, ss, sr).wait_recv()

    def gather(k, total):
        return total + SR[2 * k] + SR[2 * k + 1]
    total = lax.fori_loop(1, 16, gather, SS[c] + SR[1 - c])
    scores = total * s_ref[...].astype(F32)
    largest = jnp.max(scores, axis=0, keepdims=True)
    expo = jnp.exp(scores - largest)
    sums = jnp.sum(expo, axis=0, keepdims=True)
    weight = (expo / sums).astype(BF16)
    WS[...] = weight
    WB[c] = weight
    each(lambda k, core: send_w(k, core).start())
    ev_ref[...] = largest + jnp.log(sums)

    ACC[...] = jnp.zeros_like(ACC)
    all_of(WB, ws, wr).wait_recv()

    def accumulate(k, _):
        for core in range(2):
            ids = jnp.broadcast_to(A[2 * k + core], (64, 128))
            w = WB[2 * k + core].astype(F32)
            for m in range(16):
                WM[m * 64 : (m + 1) * 64, core * 128 : (core + 1) * 128] = jnp.where(ids == m, w, 0.0).astype(BF16)
        rows = X[pl.ds(2 * k, 2)].reshape(256, 256)
        ACC[...] += jnp.dot(WM[...], rows, preferred_element_type=F32)
        return 0
    lax.fori_loop(0, 16, accumulate, 0)

    for h in ORDER:
        p = _mod(z + h, NZ)
        RS[h] = ACC[pl.ds(pl.multiple_of(p * 128, 128), 128), :].astype(BF16)
        send_r(h).start()
    final = ACC[pl.ds(pl.multiple_of(z * 128, 128), 128), :]
    all_of(RR, rs, rr, 7).wait_recv()
    for h in range(1, NZ):
        final = final + RR[h].astype(F32)
    ASM[...] = final
    for q in range(32):
        for kk in range(2):
            FS[q, kk] = ASM[kk * 64 + 2 * q : kk * 64 + 2 * q + 2, :]
    each(lambda k, core: send_f(k, core).start())
    out_ref[:, :, cols(mine)] = FS[d]
    all_of(FS, fs, fr).wait_recv()

    for buf, sem in ((J1, js), (A, as_), (X, xs), (SS, ss), (WB, ws), (FS, fs)):
        all_of(buf, sem, sem).wait_send()
    all_of(PJ, gs, gr, 7).wait_send()
    all_of(RS, rs, rr, 7).wait_send()


def on_device(particles, assign, inv_sigma, projections):
    dma = pltpu.SemaphoreType.DMA
    vmem = pltpu.VMEM
    sums, evidence = pl.pallas_call(
        kernel,
        name="estep",
        out_shape=(
            jax.ShapeDtypeStruct((2, 2, 8192), F32),
            jax.ShapeDtypeStruct((1, 128), F32),
        ),
        in_specs=[
            pl.BlockSpec(memory_space=pl.ANY),
            pl.BlockSpec(memory_space=pltpu.VMEM),
            pl.BlockSpec(memory_space=pltpu.VMEM),
            pl.BlockSpec(memory_space=pl.ANY),
        ],
        out_specs=(
            pl.BlockSpec(memory_space=pltpu.VMEM),
            pl.BlockSpec(memory_space=pltpu.VMEM),
        ),
        scratch_shapes=[
            vmem((32, 128, 256), BF16),
            vmem((32, 1, 128), jnp.int32),
            vmem((32, 2, 2, 256), BF16),
            vmem((128, 256), F32),
            vmem((8, 128, 256), BF16),
            vmem((8, 128, 128), F32),
            vmem((1024, 256), F32),
            vmem((32, 64, 128), F32),
            vmem((32, 64, 128), F32),
            vmem((64, 128), BF16),
            vmem((32, 64, 128), BF16),
            vmem((1024, 256), BF16),
            vmem((1024, 256), F32),
            vmem((8, 128, 256), BF16),
            vmem((8, 128, 256), BF16),
            vmem((32, 2, 2, 256), F32),
            dma((2,)),
            dma, dma((16,)),
            dma, dma,
            dma, dma,
            dma, dma,
            dma, dma,
            dma, dma,
            dma, dma,
            dma, dma,
        ],
        compiler_params=pltpu.CompilerParams(collective_id=0, has_side_effects=True),
    )(particles, assign.reshape(1, 128), inv_sigma.reshape(1, 128), projections)
    return sums, evidence.reshape(128)


def solution(mesh):
    return jax.shard_map(
        on_device,
        mesh=mesh,
        in_specs=(
            P(("cls", "dom"), None),
            P(("cls", "dom"), None),
            P(("cls", "dom")),
            P("cls", "dom", None),
        ),
        out_specs=(P("cls", "dom", None), P(("cls", "dom"))),
        check_vma=False,
    )
```

time: 92 us -> 82.7 us (0.90)
  Pallas kernels: 88.5 us -> 79.2 us
    pallas_call x1, Pallas kernels: 88.5 us -> 79.2 us  [on_device(): pl.pallas_call(kernel, name='estep', out_shape=(jax.ShapeDtypeStruct((2,...]
where the time goes in v2:
time: 82.7 us; the launch traced here: 82.6 us
  Pallas kernels  79.2 us (96%)
  local copies, waits for them, and re-layouts  2.74 us (3%)
    pallas_call x1, Pallas kernels, on_device(): pl.pallas_call(kernel, name='estep', out_shape=(jax.ShapeDtypeStruct((2,...  79.2 us
    unnamed x2, local copies, waits for them, and re-layouts  2.74 us

profile of v2, /device:TPU:1, one launch (start us, length us, event | category | flops | bytes accessed | tf_op | source)
XLA Modules:
  0.0 82.6 jit_solution(15395319740878893733)
XLA Ops:
  0.6 79.2 %estep.1 = (f32[2,2,8192]{2,1,0:T(2,128)}, f32[1,128]{1,0:T(1,128)}) custom-call(bf16[128,8192]{1,0:T(8,128)(2,1)} %x_ref.1, s32[1,128]{1,0:T(1,128)} %bitcast.3, bf16[1,128]{1,0:T(2,128)(2,1)} %bitcast.4, bf16[2,2,8192]{2,1,0:T(2,128)(2,1)} %j_ref.1), custom_call_target="tpu_custom_call" | custom-call | tf_op jit(solution)/shard_map/estep/pallas_call | solution.py:282
  79.9 1.6 %copy.8 = f32[2,2,8192]{2,1,0:T(2,128)} copy(f32[2,2,8192]{2,1,0:T(2,128)} %get-tuple-element.8) | data formatting | bytes 262144
  81.4 1.2 %copy.9 = f32[128]{0:T(128)} copy(f32[128]{0:T(128)} %bitcast.5) | data formatting | bytes 1024

commit v3 on v2

--- a/solution.py
+++ b/solution.py
@@ -10,7 +10,9 @@
 MESH = pl.DeviceIdType.MESH
 TWIST = True
 EARLY = 7
-ORDER = (2, 6, 3, 5, 4, 1, 7)
+FAR_FIRST = (2, -2, 3, -3, 4, 1, -1)
+PLANES = (0, 1, -1, 2, -2, 3, -3, 4)
+SLOT = {h: q for q, h in enumerate(PLANES)}
 NX, NY, NZ = 4, 4, 8
 F32 = jnp.float32
 BF16 = jnp.bfloat16
@@ -77,7 +79,7 @@
 
     def column_peer(h):
         if TWIST:
-            return _device(x - h + 8, y - h + 8, z + h, c)
+            return _device(x - h, y - h, z + h, c)
         return _device(x, y, z + h, c)
 
     def each(fn):
@@ -138,15 +140,17 @@
     def send_w(k, core):
         return pltpu.make_async_remote_copy(
             src_ref=WS, dst_ref=WB.at[2 * k + c],
-            send_sem=ws, recv_sem=wr,
+            send_sem=ws, recv_sem=wr.at[k],
             device_id=peer(k, core), device_id_type=MESH)
 
     def send_g(h):
-        return pltpu.make_async_remote_copy(
-            src_ref=PJ.at[z], dst_ref=PJ.at[z], send_sem=gs, recv_sem=gr,
+        q = SLOT[4 if h == 4 else -h]
+        return pltpu.make_async_remote_copy(
+            src_ref=PJ.at[0], dst_ref=PJ.at[q], send_sem=gs, recv_sem=gr.at[q],
             device_id=column_peer(h), device_id_type=MESH)
 
     def send_r(h):
+        h = h % NZ
         return pltpu.make_async_remote_copy(
             src_ref=RS.at[h], dst_ref=RR.at[h], send_sem=rs, recv_sem=rr,
             device_id=column_peer(h), device_id_type=MESH)
@@ -180,23 +184,35 @@
     for q in range(32):
         for kk in range(2):
             ASM[kk * 64 + 2 * q : kk * 64 + 2 * q + 2, :] = J1[q, kk].astype(F32)
-    PJ[z] = ASM[...].astype(BF16)
-    for h in ORDER:
+    PJ[0] = ASM[...].astype(BF16)
+
+    def halve(lo, hi):
+        for q in range(lo, hi):
+            v = PJ[q].astype(F32)
+            H[q] = jnp.broadcast_to(0.5 * jnp.sum(v * v, axis=1, keepdims=True), (128, 128))
+
+    for h in FAR_FIRST:
         send_g(h).start()
     start_x(EARLY, 16)
-
-    all_of(PJ, gs, gr, 7).wait_recv()
-
-    def halve(p, _):
-        v = PJ[p].astype(F32)
-        half = 0.5 * jnp.sum(v * v, axis=1, keepdims=True)
-        H[p] = jnp.broadcast_to(half, (128, 128))
-        return 0
-    lax.fori_loop(0, NZ, halve, 0)
+    halve(0, 1)
+    for h in FAR_FIRST:
+        send_g(h).wait_recv()
+        q = SLOT[4 if h == 4 else -h]
+        halve(q, q + 1)
 
     own_x.wait()
 
     all_of(A, as_, ar).wait_recv()
+
+    def choose(total, k, core, lo, hi):
+        ids = jnp.broadcast_to(A[2 * k + core], (64, 128))
+        for q in range(lo, hi):
+            for kk in range(2):
+                at = (q - lo) * 128 + kk * 64
+                part = T[at : at + 64, core * 128 : (core + 1) * 128]
+                half = H[q, kk * 64 : kk * 64 + 64, :]
+                total = jnp.where(ids == 2 * ((z + PLANES[q]) & 7) + kk, part - half, total)
+        return total
 
     def score(k, _):
         @pl.when(k == 0)
@@ -211,13 +227,7 @@
         T[...] = lax.dot_general(
             PJ[...].reshape(1024, 256), rows, (((1,), (1,)), ((), ())), preferred_element_type=F32)
         for core in range(2):
-            ids = jnp.broadcast_to(A[2 * k + core], (64, 128))
-            total = jnp.zeros((64, 128), F32)
-            for m in range(16):
-                part = T[m * 64 : (m + 1) * 64, core * 128 : (core + 1) * 128]
-                half = H[m // 2, (m % 2) * 64 : (m % 2) * 64 + 64, :]
-                total = jnp.where(ids == m, part - half, total)
-            SS[2 * k + core] = total
+            SS[2 * k + core] = choose(jnp.zeros((64, 128), F32), k, core, 0, 8)
         for core in range(2):
             @pl.when((k != 0) | (c != core))
             def _():
@@ -240,25 +250,37 @@
     each(lambda k, core: send_w(k, core).start())
     ev_ref[...] = largest + jnp.log(sums)
 
+    def accumulate(n, group, wait):
+        for k in (2 * n, 2 * n + 1):
+            if wait:
+                @pl.when(k == 0)
+                def _():
+                    all_of(WB, ws, wr.at[0], 1).wait_recv()
+
+                @pl.when(k != 0)
+                def _():
+                    all_of(WB, ws, wr.at[k], 2).wait_recv()
+        for part in range(4):
+            ids = jnp.broadcast_to(A[4 * n + part], (64, 128))
+            w = WB[4 * n + part].astype(F32)
+            for q in range(4):
+                for kk in range(2):
+                    at = q * 128 + kk * 64
+                    live = ids == 2 * ((z + PLANES[4 * group + q]) & 7) + kk
+                    WM[at : at + 64, part * 128 : (part + 1) * 128] = jnp.where(live, w, 0.0).astype(BF16)
+        rows = X[pl.ds(4 * n, 4)].reshape(512, 256)
+        ACC[group] += jnp.dot(WM[...], rows, preferred_element_type=F32)
+        return 0
+
     ACC[...] = jnp.zeros_like(ACC)
-    all_of(WB, ws, wr).wait_recv()
-
-    def accumulate(k, _):
-        for core in range(2):
-            ids = jnp.broadcast_to(A[2 * k + core], (64, 128))
-            w = WB[2 * k + core].astype(F32)
-            for m in range(16):
-                WM[m * 64 : (m + 1) * 64, core * 128 : (core + 1) * 128] = jnp.where(ids == m, w, 0.0).astype(BF16)
-        rows = X[pl.ds(2 * k, 2)].reshape(256, 256)
-        ACC[...] += jnp.dot(WM[...], rows, preferred_element_type=F32)
-        return 0
-    lax.fori_loop(0, 16, accumulate, 0)
-
-    for h in ORDER:
-        p = _mod(z + h, NZ)
-        RS[h] = ACC[pl.ds(pl.multiple_of(p * 128, 128), 128), :].astype(BF16)
-        send_r(h).start()
-    final = ACC[pl.ds(pl.multiple_of(z * 128, 128), 128), :]
+    for group in (1, 0):
+        lax.fori_loop(0, 8, lambda n, _, group=group: accumulate(n, group, group == 1), 0)
+        for q in (3, 2, 1, 0):
+            h = PLANES[4 * group + q]
+            if h:
+                RS[h % NZ] = ACC[group, q * 128 : (q + 1) * 128, :].astype(BF16)
+                send_r(h).start()
+    final = ACC[0, 0:128, :]
     all_of(RR, rs, rr, 7).wait_recv()
     for h in range(1, NZ):
         final = final + RR[h].astype(F32)
@@ -272,8 +294,13 @@
 
     for buf, sem in ((J1, js), (A, as_), (X, xs), (SS, ss), (WB, ws), (FS, fs)):
         all_of(buf, sem, sem).wait_send()
-    all_of(PJ, gs, gr, 7).wait_send()
+    all_of(PJ, gs, gs, 7).wait_send()
     all_of(RS, rs, rr, 7).wait_send()
+
+
+def deliver(sums_ref, evidence_ref, out_ref, ev_ref):
+    out_ref[...] = sums_ref[...]
+    ev_ref[...] = evidence_ref[...]
 
 
 def on_device(particles, assign, inv_sigma, projections):
@@ -308,8 +335,8 @@
             vmem((32, 64, 128), F32),
             vmem((64, 128), BF16),
             vmem((32, 64, 128), BF16),
-            vmem((1024, 256), BF16),
-            vmem((1024, 256), F32),
+            vmem((512, 512), BF16),
+            vmem((2, 512, 256), F32),
             vmem((8, 128, 256), BF16),
             vmem((8, 128, 256), BF16),
             vmem((32, 2, 2, 256), F32),
@@ -317,14 +344,22 @@
             dma, dma((16,)),
             dma, dma,
             dma, dma,
-            dma, dma,
-            dma, dma,
-            dma, dma,
+            dma, dma((8,)),
+            dma, dma,
+            dma, dma((16,)),
             dma, dma,
             dma, dma,
         ],
         compiler_params=pltpu.CompilerParams(collective_id=0, has_side_effects=True),
     )(particles, assign.reshape(1, 128), inv_sigma.reshape(1, 128), projections)
+    sums, evidence = pl.pallas_call(
+        deliver,
+        name="deliver",
+        out_shape=(
+            jax.ShapeDtypeStruct((2, 2, 8192), F32),
+            jax.ShapeDtypeStruct((1, 128), F32),
+        ),
+    )(sums, evidence)
     return sums, evidence.reshape(128)
 
 

time: 82.7 us -> 79.3 us (0.959)
  local copies, waits for them, and re-layouts: 2.74 us -> 0 us
    unnamed x2 -> x0, local copies, waits for them, and re-layouts: 2.74 us -> none
    pallas_call x1, Pallas kernels: 79.2 us -> 76.9 us  [on_device(): pl.pallas_call(kernel, name='estep', out_shape=(jax.ShapeDtypeStruct((2,...]
    pallas_call x0 -> x1, Pallas kernels: none -> 1.57 us  [on_device(): pl.pallas_call(deliver, name='deliver', out_shape=(jax.ShapeDtypeStruct((...]
where the time goes in v3:
time: 79.3 us; the launch traced here: 79.1 us
  Pallas kernels  78.5 us (99%)
    pallas_call x1, Pallas kernels, on_device(): pl.pallas_call(kernel, name='estep', out_shape=(jax.ShapeDtypeStruct((2,...  76.9 us

profile of v3, /device:TPU:1, one launch (start us, length us, event | category | flops | bytes accessed | tf_op | source)
XLA Modules:
  0.0 79.1 jit_solution(14882517706365814571)
XLA Ops:
  0.6 76.9 %estep.1 = (f32[2,2,8192]{2,1,0:T(2,128)}, f32[1,128]{1,0:T(1,128)}) custom-call(bf16[128,8192]{1,0:T(8,128)(2,1)} %x_ref.1, s32[1,128]{1,0:T(1,128)} %bitcast.3, bf16[1,128]{1,0:T(2,128)(2,1)} %bitcast.4, bf16[2,2,8192]{2,1,0:T(2,128)(2,1)} %j_ref.1), custom_call_target="tpu_custom_call" | custom-call | tf_op jit(solution)/shard_map/estep/pallas_call | solution.py:309
  77.6 1.6 %deliver.1 = (f32[2,2,8192]{2,1,0:T(2,128)}, f32[1,128]{1,0:T(1,128)}) custom-call(f32[2,2,8192]{2,1,0:T(2,128)} %get-tuple-element.6.sums_ref, f32[1,128]{1,0:T(1,128)} %get-tuple-element.7.evidence_ref), custom_call_target="tpu_custom_call" | custom-call | tf_op jit(solution)/shard_map/deliver/pallas_call | solution.py:355

commit v4 on v3

--- a/solution.py
+++ b/solution.py
@@ -11,7 +11,7 @@
 TWIST = True
 EARLY = 7
 FAR_FIRST = (2, -2, 3, -3, 4, 1, -1)
-PLANES = (0, 1, -1, 2, -2, 3, -3, 4)
+PLANES = (0, 1, -1, 4, 2, -2, 3, -3)
 SLOT = {h: q for q, h in enumerate(PLANES)}
 NX, NY, NZ = 4, 4, 8
 F32 = jnp.float32
@@ -205,13 +205,15 @@
     all_of(A, as_, ar).wait_recv()
 
     def choose(total, k, core, lo, hi):
-        ids = jnp.broadcast_to(A[2 * k + core], (64, 128))
+        ids = jnp.broadcast_to(A[2 * k + core], (8, 128))
         for q in range(lo, hi):
             for kk in range(2):
-                at = (q - lo) * 128 + kk * 64
-                part = T[at : at + 64, core * 128 : (core + 1) * 128]
-                half = H[q, kk * 64 : kk * 64 + 64, :]
-                total = jnp.where(ids == 2 * ((z + PLANES[q]) & 7) + kk, part - half, total)
+                live = ids == 2 * ((z + PLANES[q]) & 7) + kk
+                for g in range(8):
+                    at = (q - lo) * 128 + kk * 64 + 8 * g
+                    part = T[at : at + 8, core * 128 : (core + 1) * 128]
+                    half = H[q, kk * 64 + 8 * g : kk * 64 + 8 * g + 8, :]
+                    total[g] = jnp.where(live, part - half, total[g])
         return total
 
     def score(k, _):
@@ -227,7 +229,9 @@
         T[...] = lax.dot_general(
             PJ[...].reshape(1024, 256), rows, (((1,), (1,)), ((), ())), preferred_element_type=F32)
         for core in range(2):
-            SS[2 * k + core] = choose(jnp.zeros((64, 128), F32), k, core, 0, 8)
+            total = choose([jnp.zeros((8, 128), F32)] * 8, k, core, 0, 8)
+            for g in range(8):
+                SS[2 * k + core, 8 * g : 8 * g + 8, :] = total[g]
         for core in range(2):
             @pl.when((k != 0) | (c != core))
             def _():
@@ -261,13 +265,16 @@
                 def _():
                     all_of(WB, ws, wr.at[k], 2).wait_recv()
         for part in range(4):
-            ids = jnp.broadcast_to(A[4 * n + part], (64, 128))
+            ids = jnp.broadcast_to(A[4 * n + part], (8, 128))
             w = WB[4 * n + part].astype(F32)
             for q in range(4):
                 for kk in range(2):
                     at = q * 128 + kk * 64
                     live = ids == 2 * ((z + PLANES[4 * group + q]) & 7) + kk
-                    WM[at : at + 64, part * 128 : (part + 1) * 128] = jnp.where(live, w, 0.0).astype(BF16)
+                    for g in range(4):
+                        pair = [jnp.where(live, w[16 * g + 8 * i : 16 * g + 8 * i + 8], 0.0) for i in range(2)]
+                        WM[at + 16 * g : at + 16 * g + 16, part * 128 : (part + 1) * 128] = (
+                            jnp.concatenate(pair, axis=0).astype(BF16))
         rows = X[pl.ds(4 * n, 4)].reshape(512, 256)
         ACC[group] += jnp.dot(WM[...], rows, preferred_element_type=F32)
         return 0

time: 79.3 us -> 77.9 us (0.982)
  Pallas kernels: 78.5 us -> 77.1 us
    pallas_call x1, Pallas kernels: 76.9 us -> 75.5 us  [on_device(): pl.pallas_call(kernel, name='estep', out_shape=(jax.ShapeDtypeStruct((2,...]
where the time goes in v4:
time: 77.9 us; the launch traced here: 77.8 us
  Pallas kernels  77.1 us (99%)
    pallas_call x1, Pallas kernels, on_device(): pl.pallas_call(kernel, name='estep', out_shape=(jax.ShapeDtypeStruct((2,...  75.5 us
    pallas_call x1, Pallas kernels, on_device(): pl.pallas_call(deliver, name='deliver', out_shape=(jax.ShapeDtypeStruct((...  1.57 us

profile of v4, /device:TPU:1, one launch (start us, length us, event | category | flops | bytes accessed | tf_op | source)
XLA Modules:
  0.0 77.8 jit_solution(9115008548528864146)
XLA Ops:
  0.6 75.5 %estep.1 = (f32[2,2,8192]{2,1,0:T(2,128)}, f32[1,128]{1,0:T(1,128)}) custom-call(bf16[128,8192]{1,0:T(8,128)(2,1)} %x_ref.1, s32[1,128]{1,0:T(1,128)} %bitcast.3, bf16[1,128]{1,0:T(2,128)(2,1)} %bitcast.4, bf16[2,2,8192]{2,1,0:T(2,128)(2,1)} %j_ref.1), custom_call_target="tpu_custom_call" | custom-call | tf_op jit(solution)/shard_map/estep/pallas_call | solution.py:316
  76.2 1.6 %deliver.1 = (f32[2,2,8192]{2,1,0:T(2,128)}, f32[1,128]{1,0:T(1,128)}) custom-call(f32[2,2,8192]{2,1,0:T(2,128)} %get-tuple-element.6.sums_ref, f32[1,128]{1,0:T(1,128)} %get-tuple-element.7.evidence_ref), custom_call_target="tpu_custom_call" | custom-call | tf_op jit(solution)/shard_map/deliver/pallas_call | solution.py:362

commit v5 on v4

--- a/solution.py
+++ b/solution.py
@@ -152,7 +152,7 @@
     def send_r(h):
         h = h % NZ
         return pltpu.make_async_remote_copy(
-            src_ref=RS.at[h], dst_ref=RR.at[h], send_sem=rs, recv_sem=rr,
+            src_ref=RS.at[h], dst_ref=RR.at[h], send_sem=rs, recv_sem=rr.at[h],
             device_id=column_peer(h), device_id_type=MESH)
 
     def send_f(k, core):
@@ -167,7 +167,6 @@
     own_j = pltpu.make_async_copy(j_ref.at[:, :, cols(mine)], J1.at[d], lsem.at[1])
     own_j.start()
     each(lambda k, core: send_j(k, core).start())
-    each(lambda k, core: send_a(k, core).start())
     own_x.start()
 
     def start_x(lo, hi):
@@ -193,6 +192,7 @@
 
     for h in FAR_FIRST:
         send_g(h).start()
+    each(lambda k, core: send_a(k, core).start())
     start_x(EARLY, 16)
     halve(0, 1)
     for h in FAR_FIRST:
@@ -288,9 +288,9 @@
                 RS[h % NZ] = ACC[group, q * 128 : (q + 1) * 128, :].astype(BF16)
                 send_r(h).start()
     final = ACC[0, 0:128, :]
-    all_of(RR, rs, rr, 7).wait_recv()
-    for h in range(1, NZ):
-        final = final + RR[h].astype(F32)
+    for h in (-3, 3, -2, 2, 4, -1, 1):
+        send_r(h).wait_recv()
+        final = final + RR[h % NZ].astype(F32)
     ASM[...] = final
     for q in range(32):
         for kk in range(2):
@@ -302,7 +302,7 @@
     for buf, sem in ((J1, js), (A, as_), (X, xs), (SS, ss), (WB, ws), (FS, fs)):
         all_of(buf, sem, sem).wait_send()
     all_of(PJ, gs, gs, 7).wait_send()
-    all_of(RS, rs, rr, 7).wait_send()
+    all_of(RS, rs, rs, 7).wait_send()
 
 
 def deliver(sums_ref, evidence_ref, out_ref, ev_ref):
@@ -354,7 +354,7 @@
             dma, dma((8,)),
             dma, dma,
             dma, dma((16,)),
-            dma, dma,
+            dma, dma((8,)),
             dma, dma,
         ],
         compiler_params=pltpu.CompilerParams(collective_id=0, has_side_effects=True),

time: 77.9 us -> 77.6 us (level)
  no operation moved by 1% of the time
where the time goes in v5:
time: 77.6 us; the launch traced here: 77.5 us
  Pallas kernels  76.8 us (99%)
    pallas_call x1, Pallas kernels, on_device(): pl.pallas_call(kernel, name='estep', out_shape=(jax.ShapeDtypeStruct((2,...  75.2 us
    pallas_call x1, Pallas kernels, on_device(): pl.pallas_call(deliver, name='deliver', out_shape=(jax.ShapeDtypeStruct((...  1.57 us

profile of v5, /device:TPU:1, one launch (start us, length us, event | category | flops | bytes accessed | tf_op | source)
XLA Modules:
  0.0 77.5 jit_solution(15804124141822344145)
XLA Ops:
  0.6 75.2 %estep.1 = (f32[2,2,8192]{2,1,0:T(2,128)}, f32[1,128]{1,0:T(1,128)}) custom-call(bf16[128,8192]{1,0:T(8,128)(2,1)} %x_ref.1, s32[1,128]{1,0:T(1,128)} %bitcast.3, bf16[1,128]{1,0:T(2,128)(2,1)} %bitcast.4, bf16[2,2,8192]{2,1,0:T(2,128)(2,1)} %j_ref.1), custom_call_target="tpu_custom_call" | custom-call | tf_op jit(solution)/shard_map/estep/pallas_call | solution.py:316
  75.9 1.6 %deliver.1 = (f32[2,2,8192]{2,1,0:T(2,128)}, f32[1,128]{1,0:T(1,128)}) custom-call(f32[2,2,8192]{2,1,0:T(2,128)} %get-tuple-element.6.sums_ref, f32[1,128]{1,0:T(1,128)} %get-tuple-element.7.evidence_ref), custom_call_target="tpu_custom_call" | custom-call | tf_op jit(solution)/shard_map/deliver/pallas_call | solution.py:362
